TPU v7x, 512 devices: a whole 4x8x8 slice. The times are simulated.
512 devices in a mesh: shard: 128 (over y, z, core), rep: 4 (over x).
Axes of the slice: x: 4, y: 8, z: 8, core: 2. Of those that a mesh axis runs over, the one named last changes fastest.
Arguments:
- memory: bfloat16 [131072, 512], P('shard'), may hold values from -4 to 4
- touch_owner: int32 [131072, 1], P(('shard', 'rep')), may hold values from 0 to 127; in each aligned block of 256 rows (0 to 255, 256 to 511, ...) at most 6 rows name the same one
- touch_row: int32 [131072], P(('shard', 'rep')), may hold values from 0 to 1023
- touch_time: int32 [131072], P(('shard', 'rep')), may hold values from 0 to 999
- src_slot: int32 [196608], P(('shard', 'rep')), may hold values from 0 to 255
- dst_slot: int32 [196608], P(('shard', 'rep')), may hold values from 0 to 255
- event_time: int32 [196608], P(('shard', 'rep')), may hold values from 1000 to 1999
- neighbour_blocks: int32 [1536, 2], P(('shard', 'rep')), may hold values from 0 to 2
- time_freq: float32 [128], replicated, may hold values from 0.001 to 1
- time_phase: float32 [128], replicated, may hold values from -3.140625 to 3.140625
- w_input: bfloat16 [512, 1536], P(None, 'rep'), may hold values from -0.25 to 0.25
- w_time: bfloat16 [128, 1536], P(None, 'rep'), may hold values from -0.5 to 0.5
- w_hidden: bfloat16 [512, 1536], P(None, 'rep'), may hold values from -0.25 to 0.25
- w_query: bfloat16 [512, 512], P(None, 'rep'), may hold values from -0.25 to 0.25
- w_keyval: bfloat16 [512, 1024], P(None, 'rep'), may hold values from -0.25 to 0.25
Outputs:
- event_embed: bfloat16 [196608, 512], P(('shard', 'rep'))
- new_memory: bfloat16 [131072, 512], P('shard')
Inputs may be any that keep to these rules, and one draw needn't show every extreme that they name: `touch_owner`: in each batch of 256 touched entries at most 6 have the same owner, and some owner has exactly 6 in every draw.
All inputs are finite; a program needn't handle non-finite values.
Results may differ from a plain program's by a relative error of at most 0.0054.
Values may be sent and summed in bfloat16 or wider, within the bound.
A program may use at most 64 MiB of HBM per device.

v0:
```python
import math

import jax
import jax.numpy as jnp
from jax import lax
from jax.sharding import PartitionSpec as P

H = 4
BLK = 128
NB = 2


def event_update(
    fetched,
    tick,
    source,
    target,
    stamp,
    listed,
    time_freq,
    time_phase,
    w_input,
    w_time,
    w_hidden,
    w_query,
    w_keyval,
):
    width = fetched.shape[1]
    count = stamp.shape[0]
    hsrc = fetched[source]
    hdst = fetched[target]
    spans = (stamp - tick[source]).astype(jnp.float32)
    encode = jnp.cos(spans[:, None] * time_freq[None, :] + time_phase[None, :]).astype(jnp.bfloat16)
    gin = jnp.dot(hdst, w_input, preferred_element_type=jnp.float32) + jnp.dot(
        encode, w_time, preferred_element_type=jnp.float32
    )
    ghid = jnp.dot(hsrc, w_hidden, preferred_element_type=jnp.float32)
    reset = jax.nn.sigmoid(gin[:, :width] + ghid[:, :width])
    update = jax.nn.sigmoid(gin[:, width : 2 * width] + ghid[:, width : 2 * width])
    fresh = jnp.tanh(gin[:, 2 * width :] + reset * ghid[:, 2 * width :])
    hold = hsrc.astype(jnp.float32)
    hnew = (1.0 - update) * fresh + update * hold
    entries = fetched.shape[0]
    counts = jax.ops.segment_sum(jnp.ones((count,), jnp.float32), source, entries)
    delta = jax.ops.segment_sum(hnew - hold, source, entries) / jnp.maximum(counts, 1.0)[:, None]
    hround = hnew.astype(jnp.bfloat16)
    query = jnp.dot(hround, w_query, preferred_element_type=jnp.float32).astype(jnp.bfloat16)
    keyval = jnp.dot(hdst, w_keyval, preferred_element_type=jnp.float32).astype(jnp.bfloat16)
    blocks = count // BLK
    headsz = width // H
    query4 = query.reshape(blocks, BLK, H, headsz)
    keys = (
        keyval[:, :width]
        .reshape(blocks, BLK, H, headsz)[listed]
        .reshape(blocks, NB * BLK, H, headsz)
    )
    values = (
        keyval[:, width:]
        .reshape(blocks, BLK, H, headsz)[listed]
        .reshape(blocks, NB * BLK, H, headsz)
    )
    scores = jnp.einsum(
        "qihd,qjhd->qhij", query4, keys, preferred_element_type=jnp.float32
    ) / math.sqrt(headsz)
    prob = jax.nn.softmax(scores, axis=-1).astype(jnp.bfloat16)
    attend = jnp.einsum(
        "qhij,qjhd->qihd", prob, values, preferred_element_type=jnp.float32
    ).reshape(count, width)
    embed = (hnew + attend).astype(jnp.bfloat16)
    return (embed, delta)


def shards(
    memory,
    touch_owner,
    touch_row,
    touch_time,
    src_slot,
    dst_slot,
    event_time,
    neighbour_blocks,
    time_freq,
    time_phase,
    w_input,
    w_time,
    w_hidden,
    w_query,
    w_keyval,
):
    owners = lax.axis_size("shard")
    entries = touch_row.shape[0]
    stored = memory.shape[0]
    width = memory.shape[1]
    capacity = 2 * entries // owners + 2
    owner = touch_owner[:, 0]
    hits = (owner[:, None] == jnp.arange(owners, dtype=jnp.int32)[None, :]).astype(jnp.int32)
    before = jnp.cumsum(hits, axis=0) - hits
    place = jnp.sum(before * hits, axis=1)
    request = jnp.full((owners, capacity), -1, jnp.int32).at[owner, place].set(touch_row)
    asked = lax.all_to_all(request, "shard", split_axis=0, concat_axis=0, tiled=True)
    valid = asked >= 0
    safe = jnp.clip(asked, 0, stored - 1)
    served = jnp.where(valid[:, :, None], memory[safe], jnp.zeros((), jnp.bfloat16))
    returned = lax.all_to_all(served, "shard", split_axis=0, concat_axis=0, tiled=True)
    fetched = returned[owner, place]
    full_input, full_time, full_hidden, full_query, full_keyval = (
        lax.all_gather(w_input, "rep", axis=1, tiled=True),
        lax.all_gather(w_time, "rep", axis=1, tiled=True),
        lax.all_gather(w_hidden, "rep", axis=1, tiled=True),
        lax.all_gather(w_query, "rep", axis=1, tiled=True),
        lax.all_gather(w_keyval, "rep", axis=1, tiled=True),
    )
    embed, delta = event_update(
        fetched,
        touch_time,
        src_slot,
        dst_slot,
        event_time,
        neighbour_blocks,
        time_freq,
        time_phase,
        full_input,
        full_time,
        full_hidden,
        full_query,
        full_keyval,
    )
    outgoing = jnp.zeros((owners, capacity, width), jnp.float32).at[owner, place].set(delta)
    landed = lax.all_to_all(outgoing, "shard", split_axis=0, concat_axis=0, tiled=True)
    targets = jnp.where(valid, asked, stored).reshape(-1)
    owner_part = jax.ops.segment_sum(landed.reshape(-1, width), targets, stored + 1)[:stored]
    total = lax.psum(owner_part, "rep")
    new_memory = (memory.astype(jnp.float32) + total).astype(jnp.bfloat16)
    return (embed, new_memory)


def solution(mesh):
    placed = (
        P("shard", None),
        P(("shard", "rep"), None),
        P(("shard", "rep")),
        P(("shard", "rep")),
        P(("shard", "rep")),
        P(("shard", "rep")),
        P(("shard", "rep")),
        P(("shard", "rep"), None),
        P(),
        P(),
        P(None, "rep"),
        P(None, "rep"),
        P(None, "rep"),
        P(None, "rep"),
        P(None, "rep"),
    )
    return jax.shard_map(
        shards,
        mesh=mesh,
        in_specs=placed,
        out_specs=(P(("shard", "rep"), None), P("shard", None)),
        check_vma=False,
    )
```

profile of v0, /device:TPU:1, one launch (start us, length us, event | category | flops | bytes accessed | tf_op | source)
XLA Modules:
  0.0 282.8 jit_solution(5358072486782933514)
XLA Ops:
  7.2 0.7 all-gather.6.cloned.1.call-update
  7.9 0.8 copy.62
  8.7 0.2 fusion.24
  9.0 0.9 fusion.26
  10.0 0.7 or_select_fusion
  10.7 21.3 %scatter_fusion = s32[128,6]{0,1:T(8,128)S(1)} fusion(s32[128,6]{0,1:T(8,128)S(1)} %broadcast_in_dim.33, s32[256]{0:T(256)S(1)} %bitcast.45, s32[256]{0:T(256)} %param.17), kind=kCustom, calls=%fused_computation.7 | custom fusion | bytes 5120 | tf_op jit(solution)/shard_map/scatter | solution.py:99
  32.0 0.7 copy.64
  32.7 18.4 %all-to-all-start = ((s32[128,1,6]{2,1,0:T(1,128)}), s32[128,1,6]{2,1,0:T(1,128)S(1)}, u32[]{:S(2)}, u32[]{:S(2)}) async-start(s32[128,1,6]{2,1,0:T(1,128)} %copy.64), calls=%async_computation | async-start | bytes 131072 | tf_op jit(solution)/shard_map/all_to_all | solution.py:100
  51.2 0.7 all-gather.4.cloned.1.call-update
  51.9 10.7 %all-to-all-done = s32[128,1,6]{2,1,0:T(1,128)S(1)} async-done(((s32[128,1,6]{2,1,0:T(1,128)}), s32[128,1,6]{2,1,0:T(1,128)S(1)}, u32[]{:S(2)}, u32[]{:S(2)}) %all-to-all-start) | async-done | bytes 3104 | tf_op jit(solution)/shard_map/all_to_all | solution.py:100
  62.7 0.1 copy.68
  62.8 0.1 reshape.120
  63.0 2.7 gather_fusion
  65.7 0.3 reshape.119
  66.0 0.1 copy.66
  66.1 1.2 broadcast_select_fusion
  67.3 5.9 %all-to-all-start.1 = ((bf16[128,6,512]{2,1,0:T(8,128)(2,1)}), bf16[128,6,512]{2,1,0:T(8,128)(2,1)S(1)}, u32[]{:S(2)}, u32[]{:S(2)}) async-start(bf16[128,6,512]{2,1,0:T(8,128)(2,1)} %broadcast_select_fusion), calls=%async_computation.1 | async-start | bytes 2097152 | tf_op jit(solution)/shard_map/all_to_all | solution.py:104
  73.3 2.8 gather_fusion.3
  76.1 3.9 %scatter_custom_fusion.2 = f32[256]{0:T(256)S(1)} fusion(s32[384]{0:T(512)S(1)} %copy-done.14, f32[384]{0:T(512)S(1)} %broadcast.178, f32[]{:T(128)} %constant.25.clone.1), kind=kCustom, calls=%fused_computation.85 | custom fusion | flops 384 | bytes 1028 | tf_op jit(solution)/shard_map/scatter-add | solution.py:44
  80.0 12.9 %all_gather.16 = bf16[128,1536]{1,0:T(8,128)(2,1)S(1)} all-gather(bf16[128,384]{1,0:T(8,128)(2,1)S(1)} %copy-done.11), channel_id=1, replica_groups=mesh['shard'=128,'rep'=4] {'rep'}, dimensions={1}, use_global_device_ids=true | all-gather | bytes 491520 | tf_op jit(solution)/shard_map/all_gather | solution.py:108
  93.0 2.5 fusion.28
  95.5 8.1 %all-to-all-done.1 = bf16[128,6,512]{2,1,0:T(8,128)(2,1)S(1)} async-done(((bf16[128,6,512]{2,1,0:T(8,128)(2,1)}), bf16[128,6,512]{2,1,0:T(8,128)(2,1)S(1)}, u32[]{:S(2)}, u32[]{:S(2)}) %all-to-all-start.1) | async-done | bytes 786464 | tf_op jit(solution)/shard_map/all_to_all | solution.py:104
  103.5 0.2 copy.69
  103.8 2.1 gather_fusion.1
  105.9 2.6 gather_fusion.4
  108.4 2.6 gather_fusion.2
  111.0 3.9 %fusion.50 = f32[384,1536]{1,0:T(8,128)} fusion(bf16[384,512]{1,0:T(8,128)(2,1)} %gather_fusion.4, bf16[512,1536]{1,0:T(8,128)(2,1)} %all-gather.6.cloned.1.call-done), kind=kOutput, calls=%fused_computation.91 | convolution fusion | flops 603979776 | bytes 4325376 | tf_op jit(solution)/shard_map/dot_general | solution.py:37
  114.9 2.4 convolution_add_fusion
  117.4 0.6 fusion.5
  118.0 0.4 copy-done.7
  118.4 3.7 %scatter_custom_fusion.1 = f32[256,512]{1,0:T(8,128)} fusion(s32[384]{0:T(512)S(1)} %copy-done.14, f32[384,512]{1,0:T(8,128)S(1)} %fusion.5, bf16[384,512]{1,0:T(8,128)(2,1)S(1)} %copy-done.7, f32[]{:T(128)} %constant.25.clone.1), kind=kCustom, calls=%fused_computation.28 | custom fusion | flops 589824 | bytes 1703940 | tf_op jit(solution)/shard_map/scatter-add | solution.py:45
  122.0 1.1 broadcast_divide_fusion
  123.2 0.2 broadcast_in_dim.69
  123.4 13.0 %scatter_fusion.1 = f32[128,6,512]{2,0,1:T(8,128)S(1)} fusion(f32[128,6,512]{2,0,1:T(8,128)S(1)} %broadcast_in_dim.69, s32[256]{0:T(256)S(1)} %bitcast.46, f32[256,512]{1,0:T(8,128)S(1)} %broadcast_divide_fusion), kind=kCustom, calls=%fused_computation.10 | custom fusion | bytes 1574912 | tf_op jit(solution)/shard_map/scatter | solution.py:128
  136.4 2.3 copy.79
  138.7 7.8 %all-to-all-start.2 = ((f32[128,6,512]{2,1,0:T(8,128)}), f32[128,6,512]{2,1,0:T(8,128)S(1)}, u32[]{:S(2)}, u32[]{:S(2)}) async-start(f32[128,6,512]{2,1,0:T(8,128)} %copy.79), calls=%async_computation.2 | async-start | bytes 4194304 | tf_op jit(solution)/shard_map/all_to_all | solution.py:129
  146.6 0.7 all-gather.8.cloned.1.call-update
  147.3 0.1 copy.70
  147.4 0.1 reshape.158
  147.5 0.5 broadcast.244
  148.0 0.8 reduce.5
  148.8 0.1 all_to_all.17
  149.0 49.7 %all-to-all-done.2 = f32[128,6,512]{2,1,0:T(8,128)S(1)} async-done(((f32[128,6,512]{2,1,0:T(8,128)}), f32[128,6,512]{2,1,0:T(8,128)S(1)}, u32[]{:S(2)}, u32[]{:S(2)}) %all-to-all-start.2) | async-done | bytes 1572896 | tf_op jit(solution)/shard_map/all_to_all | solution.py:129
  198.7 1.4 reshape.204
  200.0 7.7 %scatter_custom_fusion.4 = f32[1025,512]{1,0:T(8,128)S(1)} fusion(s32[768]{0:T(1024)S(1)} %fusion.37, f32[768,512]{1,0:T(8,128)} %reshape.204, f32[]{:T(128)} %constant.25.clone.1), kind=kCustom, calls=%fused_computation.22 | custom fusion | flops 393216 | bytes 2099712 | tf_op jit(solution)/shard_map/scatter-add | solution.py:131
  207.8 1.5 slice.71
  209.3 0.9 copy-done.10
  210.2 13.3 %all_gather.19 = bf16[512,512]{1,0:T(8,128)(2,1)S(1)} all-gather(bf16[512,128]{1,0:T(8,128)(2,1)S(1)} %copy-done.10), channel_id=1, replica_groups=mesh['shard'=128,'rep'=4] {'rep'}, dimensions={1}, use_global_device_ids=true | all-gather | bytes 655360 | tf_op jit(solution)/shard_map/all_gather | solution.py:110
  223.5 1.8 convolution_convert_fusion
  225.4 0.1 reshape.114
  225.6 0.7 gather_fusion.6
  226.3 0.9 copy.74
  227.2 0.1 reshape.111
  227.4 0.7 gather_fusion.5
  228.1 0.9 copy.72
  229.1 1.1 convolution_convert_fusion.1
  230.2 1.1 reshape.113
  231.3 0.9 fusion.45
  232.1 1.5 convolution_multiply_fusion
  233.7 5.2 %convolution_bitcast_fusion = f32[3,128,4,128]{1,3,2,0:T(8,128)S(1)} fusion(bf16[3,256,4,128]{3,1,0,2:T(8,128)(2,1)} %bitcast.51, f32[3,4,128]{2,1,0:T(4,128)S(1)} %fusion.45, f32[3,4,128,256]{3,2,1,0:T(8,128)} %convolution_multiply_fusion), kind=kOutput, calls=%fused_computation.20 | convolution fusion | flops 101844736 | bytes 3151872 | tf_op jit(solution)/shard_map/qhij,qjhd->qihd/dot_general | solution.py:66
  238.9 0.3 copy.78
  239.2 0.9 fusion.7
  240.1 33.2 %all-reduce.2.cloned.1.call-done = f32[1024,512]{1,0:T(8,128)} async-done(((f32[1024,512]{1,0:T(8,128)}), f32[1024,512]{1,0:T(8,128)}) %all-reduce.2.cloned.1.call-update) | async-done | bytes 2097168 | tf_op jit(solution)/shard_map/psum | solution.py:132
  273.2 3.0 %add_convert_fusion = bf16[1024,512]{1,0:T(8,128)(2,1)} fusion(f32[1024,512]{1,0:T(8,128)} %all-reduce.2.cloned.1.call-done, bf16[1024,512]{1,0:T(8,128)(2,1)S(1)} %copy-done.1), kind=kLoop, calls=%fused_computation.14 | loop fusion | flops 1572864 | bytes 4194304 | tf_op jit(solution)/shard_map/convert_element_type | solution.py:133
  (66 shorter events, 0.7 us)
Async XLA Ops:
  7.2 66.1 %copy-start = (s32[256]{0:T(256)S(1)}, s32[256]{0:T(256)}, u32[]{:S(2)}) copy-start(s32[256]{0:T(256)} %param.18) | copy-start | bytes 3076
  7.2 103.8 %all-gather.6.cloned.1.call-start = ((), (), s32[]{:S(2)}) async-start(), calls=%async_computation.4 | async-start | bytes 1966080 | tf_op jit(solution)/shard_map/all_gather | solution.py:109
  9.0 54.0 %copy-start.1 = (bf16[1024,512]{1,0:T(8,128)(2,1)S(1)}, bf16[1024,512]{1,0:T(8,128)(2,1)}, u32[]{:S(2)}) copy-start(bf16[1024,512]{1,0:T(8,128)(2,1)} %param.15) | copy-start | bytes 3145732
  32.7 29.9 %all-to-all-start = ((s32[128,1,6]{2,1,0:T(1,128)}), s32[128,1,6]{2,1,0:T(1,128)S(1)}, u32[]{:S(2)}, u32[]{:S(2)}) async-start(s32[128,1,6]{2,1,0:T(1,128)} %copy.64), calls=%async_computation | async-start | bytes 131072 | tf_op jit(solution)/shard_map/all_to_all | solution.py:100
  51.2 63.7 %all-gather.4.cloned.1.call-start = ((), (), s32[]{:S(2)}) async-start(), calls=%async_computation.3 | async-start | bytes 1966080 | tf_op jit(solution)/shard_map/all_gather | solution.py:107
  67.3 5.9 %copy-start.14 = (s32[384]{0:T(512)S(1)}, s32[384]{0:T(512)}, u32[]{:S(2)}) copy-start(s32[384]{0:T(512)} %param.19) | copy-start | bytes 4612
  67.3 36.3 %all-to-all-start.1 = ((bf16[128,6,512]{2,1,0:T(8,128)(2,1)}), bf16[128,6,512]{2,1,0:T(8,128)(2,1)S(1)}, u32[]{:S(2)}, u32[]{:S(2)}) async-start(bf16[128,6,512]{2,1,0:T(8,128)(2,1)} %broadcast_select_fusion), calls=%async_computation.1 | async-start | bytes 2097152 | tf_op jit(solution)/shard_map/all_to_all | solution.py:104
  73.2 6.8 %copy-start.13 = (s32[384]{0:T(512)S(1)}, s32[384]{0:T(512)}, u32[]{:S(2)}) copy-start(s32[384]{0:T(512)} %param.20) | copy-start | bytes 4612
  73.2 6.8 %copy-start.11 = (bf16[128,384]{1,0:T(8,128)(2,1)S(1)}, bf16[128,384]{1,0:T(8,128)(2,1)}, u32[]{:S(2)}) copy-start(bf16[128,384]{1,0:T(8,128)(2,1)} %param.26) | copy-start | bytes 294916
  73.2 19.7 %copy-start.12 = (s32[384]{0:T(512)S(1)}, s32[384]{0:T(512)}, u32[]{:S(2)}) copy-start(s32[384]{0:T(512)} %param.21) | copy-start | bytes 4612
  73.2 19.7 %copy-start.16 = (f32[128]{0:T(128)S(1)}, f32[128]{0:T(128)}, u32[]{:S(2)}) copy-start(f32[128]{0:T(128)} %param.24) | copy-start | bytes 1540
  73.2 19.7 %copy-start.17 = (f32[128]{0:T(128)S(1)}, f32[128]{0:T(128)}, u32[]{:S(2)}) copy-start(f32[128]{0:T(128)} %param.23) | copy-start | bytes 1540
  111.0 3.9 %copy-start.5 = (f32[384,1536]{1,0:T(8,128)S(1)}, f32[384,1536]{1,0:T(8,128)}, u32[]{:S(2)}) copy-start(f32[384,1536]{1,0:T(8,128)} %fusion.28) | copy-start | bytes 7077892
  114.9 2.5 copy-start.2
  114.9 2.5 copy-start.6
  117.4 1.0 copy-start.7
  118.4 3.7 %copy-start.3 = (f32[384,512]{1,0:T(8,128)}, f32[384,512]{1,0:T(8,128)S(1)}, u32[]{:S(2)}) copy-start(f32[384,512]{1,0:T(8,128)S(1)} %fusion.5) | copy-start | bytes 2359300
  138.7 8.6 %copy-start.15 = (s32[3,2]{0,1:T(2,128)S(1)}, s32[3,2]{0,1:T(2,128)}, u32[]{:S(2)}) copy-start(s32[3,2]{0,1:T(2,128)} %param.22) | copy-start | bytes 76
  138.7 60.0 %all-to-all-start.2 = ((f32[128,6,512]{2,1,0:T(8,128)}), f32[128,6,512]{2,1,0:T(8,128)S(1)}, u32[]{:S(2)}, u32[]{:S(2)}) async-start(f32[128,6,512]{2,1,0:T(8,128)} %copy.79), calls=%async_computation.2 | async-start | bytes 4194304 | tf_op jit(solution)/shard_map/all_to_all | solution.py:129
  146.5 77.0 %all-gather.8.cloned.1.call-start = ((), (), s32[]{:S(2)}) async-start(), calls=%async_computation.5 | async-start | bytes 1310720 | tf_op jit(solution)/shard_map/all_gather | solution.py:111
  147.3 126.0 %all-reduce.2.cloned.1.call-start = ((), (), s32[]{:S(2)}) async-start(), calls=%async_computation.6 | async-start | bytes 4194304 | tf_op jit(solution)/shard_map/psum | solution.py:132
  209.3 0.9 copy-start.10
  209.3 14.3 %copy-start.9 = (bf16[384,512]{1,0:T(8,128)(2,1)S(1)}, bf16[384,512]{1,0:T(8,128)(2,1)}, u32[]{:S(2)}) copy-start(bf16[384,512]{1,0:T(8,128)(2,1)} %gather_fusion.2) | copy-start | bytes 1179652
  227.4 1.7 copy-start.4
  229.0 2.2 copy-start.8
Sparse Core Ops, SparseCore 0:
  10.1 37.2 all-gather.5
  54.1 33.5 all-gather.3
  149.4 30.6 all-gather.7
  209.4 63.7 all-reduce.1
where the time goes:
time: 284 us; the launch traced here: 283 us
  waiting for transfers between devices  104 us (37%)
  local copies, waits for them, and re-layouts  62.1 us (22%)
  starting transfers between devices  32.3 us (11%)
  blocking collectives  26.2 us (9%)
  other arithmetic  24.8 us (9%)
  matrix products  19.4 us (7%)
  between operations  14.3 us (5%)
    all_to_all x1, waiting for transfers between devices, shards(): lax.all_to_all(outgoing, 'shard', split_axis=0, concat_axis=0, tiled=True)  49.7 us
    psum x1, waiting for transfers between devices, shards(): total = lax.psum(owner_part, 'rep')  33.2 us
    scatter x1, local copies, waits for them, and re-layouts, shards(): jnp.full((owners, capacity), -1, jnp.int32).at[owner, place].set(touch_row)  21.3 us
    all_to_all x1, starting transfers between devices, shards(): lax.all_to_all(request, 'shard', split_axis=0, concat_axis=0, tiled=True)  18.4 us
    scatter x2, local copies, waits for them, and re-layouts, shards(): jnp.zeros((owners, capacity, width), jnp.float32).at[owner, place]  15.3 us
    all_gather x1, blocking collectives, shards(): lax.all_gather(w_query, 'rep', axis=1, tiled=True)  13.3 us
    all_gather x1, blocking collectives, shards(): lax.all_gather(w_time, 'rep', axis=1, tiled=True)  12.9 us
    all_to_all x1, waiting for transfers between devices, shards(): lax.all_to_all(request, 'shard', split_axis=0, concat_axis=0, tiled=True)  10.7 us
  transfers between devices with their start and end apart: 7, of which 4 were waited for; matrix products, arithmetic and copies ran while one was open for 28% of the time, Pallas kernels for 0%

commit v1 on v0

v1 whole, which is shorter than its diff:
```python
import functools
import math

import jax
import jax.numpy as jnp
from jax import lax
from jax.experimental import pallas as pl
from jax.experimental.pallas import tpu as pltpu
from jax.sharding import PartitionSpec as P

H = 4
BLK = 128
LANES = 128
PAD = 8
F32 = jnp.float32
BF16 = jnp.bfloat16
I32 = jnp.int32


def mm(a, b):
    return jnp.dot(a, b, preferred_element_type=F32)


def mm_nt(a, b):
    return lax.dot_general(a, b, (((1,), (1,)), ((), ())), preferred_element_type=F32)


def mm_tn(a, b):
    return lax.dot_general(a, b, (((0,), (0,)), ((), ())), preferred_element_type=F32)


def iota(shape, dim):
    return lax.broadcasted_iota(I32, shape, dim)


def one_hot(cond):
    return jnp.where(cond, 1.0, 0.0).astype(BF16)


def column(row):
    return jnp.transpose(jnp.broadcast_to(row, (LANES, row.shape[1])))


def rowhot(col, width):
    lane = iota(col.shape, 1).astype(F32)
    parts = [one_hot(col == lane + float(k * LANES)) for k in range(pl.cdiv(width, LANES))]
    hot = parts[0] if len(parts) == 1 else jnp.concatenate(parts, axis=1)
    return hot if hot.shape[1] == width else hot[:, :width]


def body(
    n, m, cap,
    owner_ref, row_ref, tick_ref, src_ref, dst_ref, stamp_ref, listed_ref, freq_ref, phase_ref,
    mem_hbm, wi_hbm, wt_hbm, wh_hbm, wq_hbm, wk_hbm,
    embed_ref, new_ref,
    mem, wi, wt, wh, wq, wk,
    reqbuf, asked, asked_all, slots_all, served, rows, place_hot, owner_hot,
    hs, hd, hn, dsend, dall, outbuf, landed, newcol,
    local_sem, req_sem, slot_sem, ask_sem, wx_sem, wc_sem, row_sem, delta_sem, out_sem, new_sem,
):
    s = lax.axis_index("shard")
    r = lax.axis_index("rep")
    T = owner_ref.shape[1]
    E = src_ref.shape[0]
    R, D = mem.shape
    G = m * cap
    core = lax.rem(s, 2)
    sibling = s + 1 - 2 * core

    def plane(i):
        return lax.rem(s + i, n)

    def line(i):
        return lax.rem(r + i, m)

    def remote(src, dst, sems, at, shard, rep):
        return pltpu.make_async_remote_copy(
            src_ref=src, dst_ref=dst, send_sem=sems.at[(0,) + at], recv_sem=sems.at[(1,) + at],
            device_id=(shard, rep), device_id_type=pl.DeviceIdType.MESH,
        )

    def finish(ref, sem):
        pltpu.make_async_copy(ref, ref, sem).wait()

    weights = ((wi_hbm, wi), (wt_hbm, wt), (wh_hbm, wh), (wq_hbm, wq), (wk_hbm, wk))
    mem_copy = pltpu.make_async_copy(mem_hbm, mem, local_sem.at[0])
    mem_copy.start()
    own = []
    for at, (shard_ref, full) in enumerate(weights):
        width = shard_ref.shape[1]
        copy = pltpu.make_async_copy(
            shard_ref, full.at[:, pl.ds(pl.multiple_of(r * width, LANES), width)], local_sem.at[1 + at]
        )
        copy.start()
        own.append(copy)

    barrier = pltpu.get_barrier_semaphore()

    def greet(i, carry):
        pl.semaphore_signal(barrier, inc=1, device_id=(plane(i), r), device_id_type=pl.DeviceIdType.MESH)
        return carry

    lax.fori_loop(1, n, greet, 0)
    for i in range(1, m):
        pl.semaphore_signal(barrier, inc=1, device_id=(s, line(i)), device_id_type=pl.DeviceIdType.MESH)

    owner = owner_ref[...]
    hit = one_hot(iota((n, T), 0) == owner)
    earlier = one_hot(iota((T, T), 0) < iota((T, T), 1))
    place = jnp.sum(mm(hit, earlier) * hit.astype(F32), axis=0, keepdims=True)
    asked_row = row_ref[...] + 1
    line_at = iota((LANES, T), 0).astype(F32)
    ask_hi = (asked_row >> 5).astype(F32)
    ask_lo = (asked_row & 31).astype(F32)
    table = jnp.where(line_at == place, ask_hi, jnp.where(line_at == place + float(PAD), ask_lo, 0.0))
    reqbuf[...] = mm_nt(hit, table.astype(BF16)).reshape(n, 1, LANES)
    ownerf = owner.astype(F32)
    slots_all[r] = ownerf * float(G) + place + (r * cap).astype(F32)
    asked[s] = reqbuf[s]

    pl.semaphore_wait(barrier, n - 1 + m - 1)

    def ask(i, carry):
        to = plane(i)
        remote(reqbuf.at[to], asked.at[s], req_sem, (), to, r).start()
        return carry

    lax.fori_loop(1, n, ask, 0)
    for i in range(1, m):
        remote(slots_all.at[r], slots_all.at[r], slot_sem, (i,), s, line(i)).start()

    def halves(group):
        out = []
        for w in group:
            shard_ref, full = weights[w]
            depth, width = shard_ref.shape
            half = depth // 2
            out.append((w, shard_ref, full, pl.ds(pl.multiple_of(core * half, PAD), half), width))
        return out

    groups = ((1, 2, 0), (3, 4))
    for group in groups:
        for i in range(1, m):
            for w, shard_ref, full, part, width in halves(group):
                cols = pl.ds(pl.multiple_of(r * width, LANES), width)
                remote(shard_ref.at[part], full.at[part, cols], wx_sem, (w, i), s, line(i)).start()

    finish(asked.at[pl.ds(0, n - 1)], req_sem.at[1])
    table_in = asked[...].reshape(n, LANES)
    asked_all[r] = table_in
    for i in range(1, m):
        remote(asked_all.at[r], asked_all.at[r], ask_sem, (i,), s, line(i)).start()
    spread = one_hot((iota((n * PAD, n), 0) >> 3) == iota((n * PAD, n), 1))
    lane = iota((n * PAD, LANES), 1)
    mine = ((lane & (PAD - 1)) == (iota((n * PAD, LANES), 0) & (PAD - 1))) & (lane < 2 * PAD)
    picked = jnp.where(mine, mm(spread, table_in.astype(BF16)), 0.0).astype(BF16)
    depth_at = iota((LANES, LANES), 0)
    scale = jnp.where(depth_at < PAD, 32.0, jnp.where(depth_at < 2 * PAD, 1.0, 0.0)).astype(BF16)
    wanted = mm(picked, scale) - 1.0
    mem_copy.wait()
    piece = min(n * PAD, 256)
    for c in range(n * PAD // piece):
        hot = rowhot(wanted[c * piece:(c + 1) * piece], R)
        got = mm(hot, mem[...]).astype(BF16)
        served[pl.ds(c * piece // PAD, piece // PAD)] = got.reshape(piece // PAD, PAD, D)

    def serve(i, carry):
        to = plane(i)
        remote(served.at[to], rows.at[s], row_sem, (), to, r).start()
        return carry

    lax.fori_loop(1, n, serve, 0)
    rows[s] = served[s]

    src_row = src_ref[...].reshape(1, E).astype(F32)
    src_hot = rowhot(column(src_row), T)
    dst_hot = rowhot(column(dst_ref[...].reshape(1, E).astype(F32)), T)
    src_hot_t = one_hot(iota((T, E), 0).astype(F32) == src_row)
    slot_hot = rowhot(column(ownerf * float(PAD) + place), n * PAD)
    counts = mm(src_hot_t, jnp.ones((E, LANES), BF16))
    share = 1.0 / jnp.maximum(counts, 1.0)
    tick = tick_ref[...]
    tick_hi = column((tick >> 5).astype(F32)).astype(BF16)
    tick_lo = column((tick & 31).astype(F32)).astype(BF16)
    ticks = mm(src_hot, tick_hi) * 32.0 + mm(src_hot, tick_lo)
    spans = column(stamp_ref[...].reshape(1, E).astype(F32)) - ticks
    encode = jnp.cos(spans * freq_ref[...] + phase_ref[...]).astype(BF16)

    for i in range(1, m):
        finish(slots_all.at[0], slot_sem.at[1, i])
    rung = min(n * G, 384)

    def fill_place(c, carry):
        at = pl.multiple_of(c * rung, rung)
        line_no = (iota((rung, T), 0) + c * rung).astype(F32)
        for q in range(m):
            place_hot[pl.ds(at, rung), pl.ds(q * T, T)] = one_hot(line_no == slots_all[q])
        return carry

    lax.fori_loop(0, n * G // rung, fill_place, 0)

    for copy in own:
        copy.wait()

    def others(group, do):
        for i in range(1, m):
            for w, shard_ref, full, part, width in halves(group):
                cols = pl.ds(pl.multiple_of(line(i) * width, LANES), width)
                do(full.at[part, cols], w, i)

    def arrive(group):
        others(group, lambda ref, w, i: finish(ref, wx_sem.at[1, w, m - i]))
        others(group, lambda ref, w, i: remote(ref, ref, wc_sem, (w, i), sibling, r).start())

    arrive(groups[0])

    finish(rows.at[pl.ds(0, n - 1)], row_sem.at[1])
    fetched = mm(slot_hot, rows[...].reshape(n * PAD, D)).astype(BF16)
    hs[...] = mm(src_hot, fetched).astype(BF16)
    hd[...] = mm(dst_hot, fetched).astype(BF16)
    others(groups[0], lambda ref, w, i: finish(ref, wc_sem.at[1, w, i]))
    wide = 2 * LANES
    for c in range(D // wide):
        def gate(k):
            return slice(k * D + c * wide, k * D + (c + 1) * wide)
        reset = mm(hd[...], wi[:, gate(0)]) + mm(encode, wt[:, gate(0)]) + mm(hs[...], wh[:, gate(0)])
        update = mm(hd[...], wi[:, gate(1)]) + mm(encode, wt[:, gate(1)]) + mm(hs[...], wh[:, gate(1)])
        reset = 0.5 * jnp.tanh(0.5 * reset) + 0.5
        update = 0.5 * jnp.tanh(0.5 * update) + 0.5
        fresh = jnp.tanh(
            mm(hd[...], wi[:, gate(2)]) + mm(encode, wt[:, gate(2)]) + reset * mm(hs[...], wh[:, gate(2)])
        )
        hold = hs[:, c * wide:(c + 1) * wide].astype(F32)
        change = (1.0 - update) * (fresh - hold)
        hn[:, c * wide:(c + 1) * wide] = hold + change
        delta = mm(src_hot_t, change.astype(BF16))
        for k in range(2):
            dsend[2 * c + k] = (delta[:, k * LANES:(k + 1) * LANES] * share).astype(BF16)

    for i in range(1, m):
        remote(dsend.at[line(i)], dall.at[r], delta_sem, (i,), s, line(i)).start()
    dall[r] = dsend[r]
    for i in range(1, m):
        finish(dall.at[0], delta_sem.at[1, i])

    for c in range(n * G // rung):
        part = mm(place_hot[pl.ds(c * rung, rung)], dall[...].reshape(m * T, LANES)).astype(BF16)
        outbuf[pl.ds(c * rung // G, rung // G)] = part.reshape(rung // G, G, LANES)

    def post(i, carry):
        to = plane(i)
        remote(outbuf.at[to], landed.at[s], out_sem, (), to, r).start()
        return carry

    lax.fori_loop(1, n, post, 0)
    landed[s] = outbuf[s]

    for i in range(1, m):
        finish(asked_all.at[0], ask_sem.at[1, i])
    fan_no = jnp.floor((iota((n, n * G), 1).astype(F32) + 0.5) * (1.0 / G))
    fan = one_hot(fan_no == iota((n, n * G), 0).astype(F32))
    lane_no = iota((2 * PAD, n * G), 1).astype(F32)
    seat = lane_no - jnp.floor((lane_no + 0.5) * (1.0 / G)) * float(G)
    line_no = iota((2 * PAD, n * G), 0)
    weight = jnp.where(line_no < PAD, 32.0, 1.0)
    seat_of = (line_no & (PAD - 1)).astype(F32)
    target = jnp.full((1, n * G), -1.0, F32)
    for q in range(m):
        turned = jnp.transpose(asked_all[q])[:2 * PAD].astype(BF16)
        values = mm(turned, fan) * weight
        here = (seat == seat_of + float(q * cap)) & (seat_of < float(cap))
        target = target + jnp.sum(jnp.where(here, values, 0.0), axis=0, keepdims=True)
    step = LANES

    def fill_owner(c, carry):
        at = pl.multiple_of(c * step, step)
        owner_hot[pl.ds(at, step)] = one_hot((iota((step, n * G), 0) + c * step).astype(F32) == target)
        return carry

    lax.fori_loop(0, R // step, fill_owner, 0)

    arrive(groups[1])
    others(groups[1], lambda ref, w, i: finish(ref, wc_sem.at[1, w, i]))
    query = mm(hn[...].astype(BF16), wq[...]).astype(BF16)
    keyval = mm(hd[...], wk[...]).astype(BF16)
    head = D // H
    blocks = E // BLK
    block_no = iota((BLK, E), 1) >> 7
    for q in range(blocks):
        times = (block_no == listed_ref[0, q]).astype(F32) + (block_no == listed_ref[1, q]).astype(F32)
        seen = times > 0.0
        for h in range(H):
            cols = slice(h * head, (h + 1) * head)
            at = slice(q * BLK, (q + 1) * BLK)
            scores = mm_nt(query[at, cols], keyval[:, cols]) * (1.0 / math.sqrt(head))
            scores = jnp.where(seen, scores, -jnp.inf)
            top = jnp.max(scores, axis=1, keepdims=True)
            weighed = jnp.exp(scores - top) * times
            prob = (weighed / jnp.sum(weighed, axis=1, keepdims=True)).astype(BF16)
            attend = mm(prob, keyval[:, D + h * head:D + (h + 1) * head])
            embed_ref[at, cols] = (hn[at, cols] + attend).astype(BF16)

    finish(landed.at[pl.ds(0, n - 1)], out_sem.at[1])
    mycols = pl.ds(pl.multiple_of(r * LANES, LANES), LANES)
    step = min(R, 256)
    for c in range(R // step):
        total = mm(owner_hot[pl.ds(c * step, step)], landed[...].reshape(n * G, LANES))
        at = pl.ds(c * step, step)
        newcol[at] = (mem[at, mycols].astype(F32) + total).astype(BF16)
        for i in range(1, m):
            remote(newcol.at[at], new_ref.at[at, mycols], new_sem, (i,), s, line(i)).start()
    keep = pltpu.make_async_copy(newcol, new_ref.at[:, mycols], local_sem.at[0])
    keep.start()
    keep.wait()
    for i in range(1, m):
        finish(newcol, new_sem.at[1, i])

    finish(asked.at[pl.ds(0, n - 1)], req_sem.at[0])
    finish(rows.at[pl.ds(0, n - 1)], row_sem.at[0])
    finish(landed.at[pl.ds(0, n - 1)], out_sem.at[0])
    for i in range(1, m):
        finish(slots_all.at[0], slot_sem.at[0, i])
        finish(asked_all.at[0], ask_sem.at[0, i])
        finish(dall.at[0], delta_sem.at[0, i])
        finish(newcol, new_sem.at[0, i])
    for g in range(2):
        others(groups[g], lambda ref, w, i: finish(ref, wx_sem.at[0, w, i]))
        others(groups[g], lambda ref, w, i: finish(ref, wc_sem.at[0, w, i]))


def shards(
    memory, touch_owner, touch_row, touch_time, src_slot, dst_slot, event_time, neighbour_blocks,
    time_freq, time_phase, w_input, w_time, w_hidden, w_query, w_keyval,
):
    n = lax.axis_size("shard")
    m = lax.axis_size("rep")
    T = touch_row.shape[0]
    E = src_slot.shape[0]
    R, D = memory.shape
    cap = 2 * T // n + 2
    G = m * cap
    vmem = pl.BlockSpec(memory_space=pltpu.VMEM)
    anywhere = pl.BlockSpec(memory_space=pl.ANY)
    weights = (w_input, w_time, w_hidden, w_query, w_keyval)
    dma = pltpu.SemaphoreType.DMA
    return pl.pallas_call(
        functools.partial(body, n, m, cap),
        out_shape=(jax.ShapeDtypeStruct((E, D), BF16), jax.ShapeDtypeStruct((R, D), BF16)),
        in_specs=[vmem] * 6 + [pl.BlockSpec(memory_space=pltpu.SMEM)] + [vmem] * 2 + [anywhere] * 6,
        out_specs=(vmem, anywhere),
        scratch_shapes=[pltpu.VMEM((R, D), BF16)]
        + [pltpu.VMEM((w.shape[0], w.shape[1] * m), BF16) for w in weights]
        + [
            pltpu.VMEM((n, 1, LANES), F32),
            pltpu.VMEM((n, 1, LANES), F32),
            pltpu.VMEM((m, n, LANES), F32),
            pltpu.VMEM((m, 1, T), F32),
            pltpu.VMEM((n, PAD, D), BF16),
            pltpu.VMEM((n, PAD, D), BF16),
            pltpu.VMEM((n * G, m * T), BF16),
            pltpu.VMEM((R, n * G), BF16),
            pltpu.VMEM((E, D), BF16),
            pltpu.VMEM((E, D), BF16),
            pltpu.VMEM((E, D), F32),
            pltpu.VMEM((m, T, LANES), BF16),
            pltpu.VMEM((m, T, LANES), BF16),
            pltpu.VMEM((n, G, LANES), BF16),
            pltpu.VMEM((n, G, LANES), BF16),
            pltpu.VMEM((R, LANES), BF16),
            dma((6,)),
            dma((2,)),
            dma((2, m)),
            dma((2, m)),
            dma((2, len(weights), m)),
            dma((2, len(weights), m)),
            dma((2,)),
            dma((2, m)),
            dma((2,)),
            dma((2, m)),
        ],
        compiler_params=pltpu.CompilerParams(
            collective_id=0, has_side_effects=True, vmem_limit_bytes=56 * 1024 * 1024
        ),
    )(
        touch_owner.reshape(1, T), touch_row.reshape(1, T), touch_time.reshape(1, T),
        src_slot, dst_slot, event_time,
        neighbour_blocks.T, time_freq.reshape(1, -1), time_phase.reshape(1, -1),
        memory, *weights,
    )


def solution(mesh):
    both = P(("shard", "rep"))
    placed = (
        P("shard", None), P(("shard", "rep"), None), both, both, both, both, both,
        P(("shard", "rep"), None), P(), P(),
    ) + (P(None, "rep"),) * 5
    return jax.shard_map(
        shards,
        mesh=mesh,
        in_specs=placed,
        out_specs=(P(("shard", "rep"), None), P("shard", None)),
        check_vma=False,
    )
```

time: 284 us -> 111 us (0.39)
  Pallas kernels: 0 us -> 106 us
  waiting for transfers between devices: 104 us -> 0 us
  local copies, waits for them, and re-layouts: 62.1 us -> 4.03 us
  starting transfers between devices: 32.3 us -> 0 us
  blocking collectives: 26.2 us -> 0 us
  other arithmetic: 24.8 us -> 0 us
  matrix products: 19.4 us -> 0 us
  between operations: 14.3 us -> 0.65 us
    pallas_call x0 -> x1, Pallas kernels: none -> 106 us  [shards(): pl.pallas_call(functools.partial(body, n, m, cap), out_shape=(jax.ShapeDt...]
    all_to_all x3 -> x0, waiting for transfers between devices: 68.5 us -> none  [the longest x1 49.7 us: shards(): lax.all_to_all(outgoing, 'shard', split_axis=0, concat_axis=0, tiled=True)]
    scatter x3 -> x0, local copies, waits for them, and re-layouts: 36.6 us -> none  [the longest x1 21.3 us: shards(): jnp.full((owners, capacity), -1, jnp.int32).at[owner, place].set(touch_row)]
    psum x1 -> x0, waiting for transfers between devices: 33.2 us -> none  [shards(): total = lax.psum(owner_part, 'rep')]
    all_to_all x3 -> x0, starting transfers between devices: 32.1 us -> none  [the longest x1 18.4 us: shards(): lax.all_to_all(request, 'shard', split_axis=0, concat_axis=0, tiled=True)]
    all_gather x2 -> x0, blocking collectives: 26.2 us -> none  [the longest x1 13.3 us: shards(): lax.all_gather(w_query, 'rep', axis=1, tiled=True)]
    dot_general x7 -> x0, matrix products: 18.5 us -> none  [the longest x1 5.23 us: event_update(): jnp.einsum('qhij,qjhd->qihd', prob, values, preferred_element_type=jnp.fl...]
    gather x10 -> x0, local copies, waits for them, and re-layouts: 16.2 us -> none  [the longest x2 2.94 us: shards(): memory[safe]]
  transfers between devices with their start and end apart: 7 -> 0, of which waited for: 4 -> 0; matrix products, arithmetic and copies ran while one was open for 28% -> 0% of each run, Pallas kernels for 0% -> 0%
where the time goes in v1:
time: 111 us; the launch traced here: 110 us
  Pallas kernels  106 us (95%)
  local copies, waits for them, and re-layouts  4.03 us (4%)
    pallas_call x1, Pallas kernels, shards(): pl.pallas_call(functools.partial(body, n, m, cap), out_shape=(jax.ShapeDt...  106 us
    unnamed x2, local copies, waits for them, and re-layouts  4.03 us

profile of v1, /device:TPU:1, one launch (start us, length us, event | category | flops | bytes accessed | tf_op | source)
XLA Modules:
  0.0 110.4 jit_solution(9183517727291536840)
XLA Ops:
  0.6 105.8 %shard_map.158 = (bf16[384,512]{1,0:T(8,128)(2,1)}, bf16[1024,512]{1,0:T(8,128)(2,1)}) custom-call(s32[1,256]{1,0:T(1,128)} %bitcast.6, s32[1,256]{1,0:T(1,128)} %bitcast.7, s32[1,256]{1,0:T(1,128)} %bitcast.8, s32[384]{0:T(512)} %src_ref.1, s32[384]{0:T(512)} %dst_ref.1, s32[384]{0:T(512)} %stamp_ref.1, s32[2,3]{1,0:T(2,128)} %bitcast.9, ...), custom_call_target="tpu_custom_call" | custom-call | tf_op jit(solution)/shard_map/pallas_call | solution.py:346
  106.4 1.8 %copy.19 = bf16[384,512]{1,0:T(8,128)(2,1)} copy(bf16[384,512]{1,0:T(8,128)(2,1)} %get-tuple-element.4) | data formatting | bytes 786432
  108.2 2.3 %copy.20 = bf16[1024,512]{1,0:T(8,128)(2,1)} copy(bf16[1024,512]{1,0:T(8,128)(2,1)} %get-tuple-element.5) | data formatting | bytes 2097152

commit v2 on v1

--- a/solution.py
+++ b/solution.py
@@ -12,6 +12,8 @@
 BLK = 128
 LANES = 128
 PAD = 8
+YS = 8
+CUTS = 8
 F32 = jnp.float32
 BF16 = jnp.bfloat16
 I32 = jnp.int32
@@ -54,8 +56,8 @@
     mem_hbm, wi_hbm, wt_hbm, wh_hbm, wq_hbm, wk_hbm,
     embed_ref, new_ref,
     mem, wi, wt, wh, wq, wk,
-    reqbuf, asked, asked_all, slots_all, served, rows, place_hot, owner_hot,
-    hs, hd, hn, dsend, dall, outbuf, landed, newcol,
+    reqbuf, halfway, asked, asked_all, slots_all, served, rows, place_hot, owner_hot,
+    hs, hd, hn, dsend, dall, outbuf, landed, newcol, want, slot_hot, total,
     local_sem, req_sem, slot_sem, ask_sem, wx_sem, wc_sem, row_sem, delta_sem, out_sem, new_sem,
 ):
     s = lax.axis_index("shard")
@@ -64,11 +66,9 @@
     E = src_ref.shape[0]
     R, D = mem.shape
     G = m * cap
+    W = n // YS
     core = lax.rem(s, 2)
     sibling = s + 1 - 2 * core
-
-    def plane(i):
-        return lax.rem(s + i, n)
 
     def line(i):
         return lax.rem(r + i, m)
@@ -96,13 +96,48 @@
 
     barrier = pltpu.get_barrier_semaphore()
 
+    yy = s // W
+    ww = lax.rem(s, W)
+
+    def signal(sem, shard, rep):
+        pl.semaphore_signal(sem, inc=1, device_id=(shard, rep), device_id_type=pl.DeviceIdType.MESH)
+
+    for i in range(1, YS):
+        signal(barrier, lax.rem(yy + i, YS) * W + ww, r)
+
     def greet(i, carry):
-        pl.semaphore_signal(barrier, inc=1, device_id=(plane(i), r), device_id_type=pl.DeviceIdType.MESH)
+        signal(barrier, yy * W + lax.rem(ww + i, W), r)
         return carry
 
-    lax.fori_loop(1, n, greet, 0)
-    for i in range(1, m):
-        pl.semaphore_signal(barrier, inc=1, device_id=(s, line(i)), device_id_type=pl.DeviceIdType.MESH)
+    lax.fori_loop(1, W, greet, 0)
+    for i in range(1, m):
+        signal(barrier, s, line(i))
+    rows[...] = jnp.zeros_like(rows)
+
+    half = YS // 2
+    turns = (2, 1, 3, 0)
+
+    def quarter(turn):
+        return lax.rem(yy // 2 + turn, half)
+
+    def scatter(lines, send):
+        def pick(q, carry):
+            for k, (turn, which) in enumerate(lines):
+                at = lax.rem(ww + q * 5 + k * 3 + W // 2, W)
+                to = (quarter(turn) * 2 + which) * W + at
+                if turn:
+                    send(turn, to)
+                else:
+                    pl.when(to != s)(lambda: send(turn, to))
+            return carry
+
+        lax.fori_loop(0, W, pick, 0)
+
+    first_lines = ((2, 0), (2, 1))
+    other_lines = ((1, 1), (3, 0), (1, 0), (3, 1), (0, 0), (0, 1))
+
+    def group_size(turn):
+        return 2 * W if turn else 2 * W - 1
 
     owner = owner_ref[...]
     hit = one_hot(iota((n, T), 0) == owner)
@@ -113,19 +148,25 @@
     ask_hi = (asked_row >> 5).astype(F32)
     ask_lo = (asked_row & 31).astype(F32)
     table = jnp.where(line_at == place, ask_hi, jnp.where(line_at == place + float(PAD), ask_lo, 0.0))
-    reqbuf[...] = mm_nt(hit, table.astype(BF16)).reshape(n, 1, LANES)
+    reqbuf[...] = mm_nt(hit, table.astype(BF16)).reshape(YS, W, 1, LANES)
     ownerf = owner.astype(F32)
     slots_all[r] = ownerf * float(G) + place + (r * cap).astype(F32)
-    asked[s] = reqbuf[s]
-
-    pl.semaphore_wait(barrier, n - 1 + m - 1)
+    halfway[yy] = reqbuf[yy]
+
+    pl.semaphore_wait(barrier, YS - 1 + W - 1 + m - 1)
+
+    for i in range(1, YS):
+        y = lax.rem(yy + i, YS)
+        remote(reqbuf.at[y], halfway.at[yy], req_sem, (0,), y * W + ww, r).start()
+    finish(halfway.at[pl.ds(0, YS - 1)], req_sem.at[1, 0])
 
     def ask(i, carry):
-        to = plane(i)
-        remote(reqbuf.at[to], asked.at[s], req_sem, (), to, r).start()
+        w = lax.rem(ww + i, W)
+        remote(halfway.at[:, w], asked.at[:, ww], req_sem, (1,), yy * W + w, r).start()
         return carry
 
-    lax.fori_loop(1, n, ask, 0)
+    lax.fori_loop(1, W, ask, 0)
+    asked[:, ww] = halfway[:, ww]
     for i in range(1, m):
         remote(slots_all.at[r], slots_all.at[r], slot_sem, (i,), s, line(i)).start()
 
@@ -139,13 +180,16 @@
         return out
 
     groups = ((1, 2, 0), (3, 4))
-    for group in groups:
+
+    def give(group):
         for i in range(1, m):
             for w, shard_ref, full, part, width in halves(group):
                 cols = pl.ds(pl.multiple_of(r * width, LANES), width)
                 remote(shard_ref.at[part], full.at[part, cols], wx_sem, (w, i), s, line(i)).start()
 
-    finish(asked.at[pl.ds(0, n - 1)], req_sem.at[1])
+    give(groups[0])
+
+    finish(asked.at[:, pl.ds(0, W - 1)], req_sem.at[1, 1])
     table_in = asked[...].reshape(n, LANES)
     asked_all[r] = table_in
     for i in range(1, m):
@@ -156,27 +200,27 @@
     picked = jnp.where(mine, mm(spread, table_in.astype(BF16)), 0.0).astype(BF16)
     depth_at = iota((LANES, LANES), 0)
     scale = jnp.where(depth_at < PAD, 32.0, jnp.where(depth_at < 2 * PAD, 1.0, 0.0)).astype(BF16)
-    wanted = mm(picked, scale) - 1.0
+    want[...] = mm(picked, scale) - 1.0
     mem_copy.wait()
-    piece = min(n * PAD, 256)
-    for c in range(n * PAD // piece):
-        hot = rowhot(wanted[c * piece:(c + 1) * piece], R)
-        got = mm(hot, mem[...]).astype(BF16)
-        served[pl.ds(c * piece // PAD, piece // PAD)] = got.reshape(piece // PAD, PAD, D)
-
-    def serve(i, carry):
-        to = plane(i)
-        remote(served.at[to], rows.at[s], row_sem, (), to, r).start()
-        return carry
-
-    lax.fori_loop(1, n, serve, 0)
+    piece = 2 * W * PAD
+
+    def serve(turn, to):
+        remote(served.at[to, pl.ds(0, cap)], rows.at[s, pl.ds(0, cap)], row_sem, (turn,), to, r).start()
+
+    for turn in turns:
+        first = quarter(turn) * 2 * W
+        hot = rowhot(want[pl.ds(pl.multiple_of(first * PAD, piece), piece)], R)
+        served[pl.ds(first, 2 * W)] = mm(hot, mem[...]).astype(BF16).reshape(2 * W, PAD, D)
+        if turn == turns[0]:
+            scatter(first_lines, serve)
+    scatter(other_lines, serve)
     rows[s] = served[s]
 
     src_row = src_ref[...].reshape(1, E).astype(F32)
     src_hot = rowhot(column(src_row), T)
     dst_hot = rowhot(column(dst_ref[...].reshape(1, E).astype(F32)), T)
     src_hot_t = one_hot(iota((T, E), 0).astype(F32) == src_row)
-    slot_hot = rowhot(column(ownerf * float(PAD) + place), n * PAD)
+    slot_hot[...] = rowhot(column(ownerf * float(PAD) + place), n * PAD)
     counts = mm(src_hot_t, jnp.ones((E, LANES), BF16))
     share = 1.0 / jnp.maximum(counts, 1.0)
     tick = tick_ref[...]
@@ -214,12 +258,24 @@
 
     arrive(groups[0])
 
-    finish(rows.at[pl.ds(0, n - 1)], row_sem.at[1])
-    fetched = mm(slot_hot, rows[...].reshape(n * PAD, D)).astype(BF16)
+    fetched = jnp.zeros((T, D), F32)
+    for turn in turns:
+        finish(rows.at[pl.ds(0, group_size(turn)), pl.ds(0, cap)], row_sem.at[1, turn])
+        first = quarter(half - turn) * 2 * W
+        came = slot_hot[:, pl.ds(pl.multiple_of(first * PAD, piece), piece)]
+        fetched = fetched + mm(came, rows[pl.ds(first, 2 * W)].reshape(piece, D))
+    fetched = fetched.astype(BF16)
     hs[...] = mm(src_hot, fetched).astype(BF16)
     hd[...] = mm(dst_hot, fetched).astype(BF16)
     others(groups[0], lambda ref, w, i: finish(ref, wc_sem.at[1, w, i]))
     wide = 2 * LANES
+
+    def delta_copy(to):
+        return pltpu.make_async_remote_copy(
+            src_ref=dsend.at[to], dst_ref=dall.at[r], send_sem=delta_sem.at[0, to], recv_sem=delta_sem.at[1, r],
+            device_id=(s, to), device_id_type=pl.DeviceIdType.MESH,
+        )
+
     for c in range(D // wide):
         def gate(k):
             return slice(k * D + c * wide, k * D + (c + 1) * wide)
@@ -235,24 +291,29 @@
         hn[:, c * wide:(c + 1) * wide] = hold + change
         delta = mm(src_hot_t, change.astype(BF16))
         for k in range(2):
-            dsend[2 * c + k] = (delta[:, k * LANES:(k + 1) * LANES] * share).astype(BF16)
-
-    for i in range(1, m):
-        remote(dsend.at[line(i)], dall.at[r], delta_sem, (i,), s, line(i)).start()
+            to = 2 * c + k
+            dsend[to] = (delta[:, k * LANES:(k + 1) * LANES] * share).astype(BF16)
+
+            @pl.when(r != to)
+            def _():
+                delta_copy(to).start()
+
     dall[r] = dsend[r]
     for i in range(1, m):
-        finish(dall.at[0], delta_sem.at[1, i])
-
-    for c in range(n * G // rung):
-        part = mm(place_hot[pl.ds(c * rung, rung)], dall[...].reshape(m * T, LANES)).astype(BF16)
-        outbuf[pl.ds(c * rung // G, rung // G)] = part.reshape(rung // G, G, LANES)
-
-    def post(i, carry):
-        to = plane(i)
-        remote(outbuf.at[to], landed.at[s], out_sem, (), to, r).start()
-        return carry
-
-    lax.fori_loop(1, n, post, 0)
+        finish(dall.at[0], delta_sem.at[1, line(i)])
+    give(groups[1])
+
+    def post(turn, to):
+        remote(outbuf.at[to], landed.at[s], out_sem, (turn,), to, r).start()
+
+    span = 2 * W * G
+    for turn in turns:
+        first = quarter(turn) * 2 * W
+        part = mm(place_hot[pl.ds(pl.multiple_of(first * G, span), span)], dall[...].reshape(m * T, LANES))
+        outbuf[pl.ds(first, 2 * W)] = part.astype(BF16).reshape(2 * W, G, LANES)
+        if turn == turns[0]:
+            scatter(first_lines, post)
+    scatter(other_lines, post)
     landed[s] = outbuf[s]
 
     for i in range(1, m):
@@ -300,32 +361,80 @@
             attend = mm(prob, keyval[:, D + h * head:D + (h + 1) * head])
             embed_ref[at, cols] = (hn[at, cols] + attend).astype(BF16)
 
-    finish(landed.at[pl.ds(0, n - 1)], out_sem.at[1])
-    mycols = pl.ds(pl.multiple_of(r * LANES, LANES), LANES)
-    step = min(R, 256)
-    for c in range(R // step):
-        total = mm(owner_hot[pl.ds(c * step, step)], landed[...].reshape(n * G, LANES))
+    def cols_of(rep):
+        return pl.ds(pl.multiple_of(rep * LANES, LANES), LANES)
+
+    def landed_part(turn, lines):
+        first = quarter(half - turn) * 2 * W
+        hot = owner_hot[lines, pl.ds(pl.multiple_of(first * G, span), span)]
+        return mm(hot, landed[pl.ds(first, 2 * W)].reshape(span, LANES))
+
+    right, left = line(1), line(m - 1)
+    for turn in turns[:-1]:
+        finish(landed.at[pl.ds(0, group_size(turn))], out_sem.at[1, turn])
+        part = landed_part(turn, slice(None))
+        total[...] = part if turn == turns[0] else total[...] + part
+    turn = turns[-1]
+    finish(landed.at[pl.ds(0, group_size(turn))], out_sem.at[1, turn])
+    step = R // CUTS
+
+    def new_copy(kind, c, src, owner_rep, to):
+        at = (pl.ds(c * step, step), cols_of(owner_rep))
+        return remote(new_ref.at[at] if src is None else src, new_ref.at[at], new_sem, (kind, c), s, to)
+
+    for c in range(CUTS):
         at = pl.ds(c * step, step)
-        newcol[at] = (mem[at, mycols].astype(F32) + total).astype(BF16)
-        for i in range(1, m):
-            remote(newcol.at[at], new_ref.at[at, mycols], new_sem, (i,), s, line(i)).start()
-    keep = pltpu.make_async_copy(newcol, new_ref.at[:, mycols], local_sem.at[0])
+        newcol[at] = (mem[at, cols_of(r)].astype(F32) + (total[at] + landed_part(turn, at))).astype(BF16)
+        new_copy(0, c, newcol.at[at], r, right).start()
+        new_copy(1, c, newcol.at[at], r, left).start()
+    keep = pltpu.make_async_copy(newcol, new_ref.at[:, cols_of(r)], local_sem.at[0])
     keep.start()
+    for c in range(CUTS):
+        if c % 2 == 0:
+            finish(newcol.at[pl.ds(0, step)], new_sem.at[1, 0, c])
+            new_copy(2, c, None, left, right).start()
+        else:
+            finish(newcol.at[pl.ds(0, step)], new_sem.at[1, 1, c])
+            new_copy(3, c, None, right, left).start()
     keep.wait()
-    for i in range(1, m):
-        finish(newcol, new_sem.at[1, i])
-
-    finish(asked.at[pl.ds(0, n - 1)], req_sem.at[0])
-    finish(rows.at[pl.ds(0, n - 1)], row_sem.at[0])
-    finish(landed.at[pl.ds(0, n - 1)], out_sem.at[0])
+    for c in range(CUTS):
+        finish(newcol.at[pl.ds(0, step)], new_sem.at[1, 1 - c % 2, c])
+        finish(newcol.at[pl.ds(0, step)], new_sem.at[1, 2 + c % 2, c])
+
+    finish(halfway.at[pl.ds(0, YS - 1)], req_sem.at[0, 0])
+    finish(asked.at[:, pl.ds(0, W - 1)], req_sem.at[0, 1])
+    for turn in turns:
+        finish(rows.at[pl.ds(0, group_size(turn)), pl.ds(0, cap)], row_sem.at[0, turn])
+        finish(landed.at[pl.ds(0, group_size(turn))], out_sem.at[0, turn])
+    for c in range(CUTS):
+        for kind in (0, 1, 2 + c % 2):
+            finish(newcol.at[pl.ds(0, step)], new_sem.at[0, kind, c])
     for i in range(1, m):
         finish(slots_all.at[0], slot_sem.at[0, i])
         finish(asked_all.at[0], ask_sem.at[0, i])
-        finish(dall.at[0], delta_sem.at[0, i])
-        finish(newcol, new_sem.at[0, i])
+        finish(dall.at[0], delta_sem.at[0, line(i)])
     for g in range(2):
         others(groups[g], lambda ref, w, i: finish(ref, wx_sem.at[0, w, i]))
         others(groups[g], lambda ref, w, i: finish(ref, wc_sem.at[0, w, i]))
+
+
+def settle(embed_in, new_in, embed_out, new_out, embed_buf, new_buf, sems):
+    moves = []
+    for src, buf, dst, count in ((new_in, new_buf, new_out, 4), (embed_in, embed_buf, embed_out, 2)):
+        size = src.shape[0] // count
+        for c in range(count):
+            at = pl.ds(c * size, size)
+            k = len(moves)
+            moves.append((
+                pltpu.make_async_copy(src.at[at], buf.at[at], sems.at[0, k]),
+                pltpu.make_async_copy(buf.at[at], dst.at[at], sems.at[1, k]),
+            ))
+            moves[-1][0].start()
+    for come, go in moves:
+        come.wait()
+        go.start()
+    for come, go in moves:
+        go.wait()
 
 
 def shards(
@@ -343,7 +452,7 @@
     anywhere = pl.BlockSpec(memory_space=pl.ANY)
     weights = (w_input, w_time, w_hidden, w_query, w_keyval)
     dma = pltpu.SemaphoreType.DMA
-    return pl.pallas_call(
+    embed, new_memory = pl.pallas_call(
         functools.partial(body, n, m, cap),
         out_shape=(jax.ShapeDtypeStruct((E, D), BF16), jax.ShapeDtypeStruct((R, D), BF16)),
         in_specs=[vmem] * 6 + [pl.BlockSpec(memory_space=pltpu.SMEM)] + [vmem] * 2 + [anywhere] * 6,
@@ -351,8 +460,9 @@
         scratch_shapes=[pltpu.VMEM((R, D), BF16)]
         + [pltpu.VMEM((w.shape[0], w.shape[1] * m), BF16) for w in weights]
         + [
-            pltpu.VMEM((n, 1, LANES), F32),
-            pltpu.VMEM((n, 1, LANES), F32),
+            pltpu.VMEM((YS, n // YS, 1, LANES), F32),
+            pltpu.VMEM((YS, n // YS, 1, LANES), F32),
+            pltpu.VMEM((YS, n // YS, 1, LANES), F32),
             pltpu.VMEM((m, n, LANES), F32),
             pltpu.VMEM((m, 1, T), F32),
             pltpu.VMEM((n, PAD, D), BF16),
@@ -367,16 +477,19 @@
             pltpu.VMEM((n, G, LANES), BF16),
             pltpu.VMEM((n, G, LANES), BF16),
             pltpu.VMEM((R, LANES), BF16),
+            pltpu.VMEM((n * PAD, LANES), F32),
+            pltpu.VMEM((T, n * PAD), BF16),
+            pltpu.VMEM((R, LANES), F32),
             dma((6,)),
-            dma((2,)),
+            dma((2, 2)),
             dma((2, m)),
             dma((2, m)),
             dma((2, len(weights), m)),
             dma((2, len(weights), m)),
-            dma((2,)),
+            dma((2, YS // 2)),
             dma((2, m)),
-            dma((2,)),
-            dma((2, m)),
+            dma((2, YS // 2)),
+            dma((2, 4, CUTS)),
         ],
         compiler_params=pltpu.CompilerParams(
             collective_id=0, has_side_effects=True, vmem_limit_bytes=56 * 1024 * 1024
@@ -387,6 +500,14 @@
         neighbour_blocks.T, time_freq.reshape(1, -1), time_phase.reshape(1, -1),
         memory, *weights,
     )
+    return pl.pallas_call(
+        settle,
+        out_shape=(jax.ShapeDtypeStruct((E, D), BF16), jax.ShapeDtypeStruct((R, D), BF16)),
+        in_specs=[anywhere] * 2,
+        out_specs=(anywhere, anywhere),
+        scratch_shapes=[pltpu.VMEM((E, D), BF16), pltpu.VMEM((R, D), BF16), dma((2, 6))],
+        cost_estimate=pl.CostEstimate(flops=0, bytes_accessed=4 * (E + R) * D, transcendentals=0),
+    )(embed, new_memory)
 
 
 def solution(mesh):

time: 111 us -> 96.6 us (0.87)
  Pallas kernels: 106 us -> 95.6 us
  local copies, waits for them, and re-layouts: 4.03 us -> 0 us
    pallas_call x1, Pallas kernels: 106 us -> 93.5 us  [shards(): pl.pallas_call(functools.partial(body, n, m, cap), out_shape=(jax.ShapeDt...]
    unnamed x2 -> x0, local copies, waits for them, and re-layouts: 4.03 us -> none
    pallas_call x0 -> x1, Pallas kernels: none -> 2.14 us  [shards(): pl.pallas_call(settle, out_shape=(jax.ShapeDtypeStruct((E, D), BF16), jax...]
where the time goes in v2:
time: 96.6 us; the launch traced here: 96.4 us
  Pallas kernels  95.6 us (99%)
    pallas_call x1, Pallas kernels, shards(): pl.pallas_call(functools.partial(body, n, m, cap), out_shape=(jax.ShapeDt...  93.5 us
    pallas_call x1, Pallas kernels, shards(): pl.pallas_call(settle, out_shape=(jax.ShapeDtypeStruct((E, D), BF16), jax...  2.14 us

profile of v2, /device:TPU:1, one launch (start us, length us, event | category | flops | bytes accessed | tf_op | source)
XLA Modules:
  0.0 96.4 jit_solution(6800577388037561991)
XLA Ops:
  0.6 93.5 %shard_map.158 = (bf16[384,512]{1,0:T(8,128)(2,1)}, bf16[1024,512]{1,0:T(8,128)(2,1)}) custom-call(s32[1,256]{1,0:T(1,128)} %bitcast.6, s32[1,256]{1,0:T(1,128)} %bitcast.7, s32[1,256]{1,0:T(1,128)} %bitcast.8, s32[384]{0:T(512)} %src_ref.1, s32[384]{0:T(512)} %dst_ref.1, s32[384]{0:T(512)} %stamp_ref.1, s32[2,3]{1,0:T(2,128)} %bitcast.9, ...), custom_call_target="tpu_custom_call" | custom-call | tf_op jit(solution)/shard_map/pallas_call | solution.py:455
  94.1 2.1 %shard_map.159 = (bf16[384,512]{1,0:T(8,128)(2,1)}, bf16[1024,512]{1,0:T(8,128)(2,1)}) custom-call(bf16[384,512]{1,0:T(8,128)(2,1)} %get-tuple-element.4.embed_in, bf16[1024,512]{1,0:T(8,128)(2,1)} %get-tuple-element.5.new_in), custom_call_target="tpu_custom_call" | custom-call | bytes 2883584 | tf_op jit(solution)/shard_map/pallas_call | solution.py:503

commit v3 on v2

--- a/solution.py
+++ b/solution.py
@@ -52,14 +52,20 @@
 
 def body(
     n, m, cap,
-    owner_ref, row_ref, tick_ref, src_ref, dst_ref, stamp_ref, listed_ref, freq_ref, phase_ref,
-    mem_hbm, wi_hbm, wt_hbm, wh_hbm, wq_hbm, wk_hbm,
-    embed_ref, new_ref,
+    *refs,
+):
+    small_hbm, refs = refs[:9], refs[9:]
+    (
+        mem_hbm, wi_hbm, wt_hbm, wh_hbm, wq_hbm, wk_hbm, embed_hbm, new_ref,
+    ), refs = refs[:8], refs[8:]
+    small, small_sem, embed_ref, refs = refs[:9], refs[9], refs[10], refs[11:]
+    owner_ref, row_ref, tick_ref, src_ref, dst_ref, stamp_ref, listed_ref, freq_ref, phase_ref = small
+    (
     mem, wi, wt, wh, wq, wk,
     reqbuf, halfway, asked, asked_all, slots_all, served, rows, place_hot, owner_hot,
     hs, hd, hn, dsend, dall, outbuf, landed, newcol, want, slot_hot, total,
     local_sem, req_sem, slot_sem, ask_sem, wx_sem, wc_sem, row_sem, delta_sem, out_sem, new_sem,
-):
+    ) = refs
     s = lax.axis_index("shard")
     r = lax.axis_index("rep")
     T = owner_ref.shape[1]
@@ -82,6 +88,11 @@
     def finish(ref, sem):
         pltpu.make_async_copy(ref, ref, sem).wait()
 
+    small_copies = [
+        pltpu.make_async_copy(src, dst, small_sem.at[k]) for k, (src, dst) in enumerate(zip(small_hbm, small))
+    ]
+    for copy in small_copies:
+        copy.start()
     weights = ((wi_hbm, wi), (wt_hbm, wt), (wh_hbm, wh), (wq_hbm, wq), (wk_hbm, wk))
     mem_copy = pltpu.make_async_copy(mem_hbm, mem, local_sem.at[0])
     mem_copy.start()
@@ -139,6 +150,8 @@
     def group_size(turn):
         return 2 * W if turn else 2 * W - 1
 
+    for copy in small_copies[:2]:
+        copy.wait()
     owner = owner_ref[...]
     hit = one_hot(iota((n, T), 0) == owner)
     earlier = one_hot(iota((T, T), 0) < iota((T, T), 1))
@@ -191,9 +204,6 @@
 
     finish(asked.at[:, pl.ds(0, W - 1)], req_sem.at[1, 1])
     table_in = asked[...].reshape(n, LANES)
-    asked_all[r] = table_in
-    for i in range(1, m):
-        remote(asked_all.at[r], asked_all.at[r], ask_sem, (i,), s, line(i)).start()
     spread = one_hot((iota((n * PAD, n), 0) >> 3) == iota((n * PAD, n), 1))
     lane = iota((n * PAD, LANES), 1)
     mine = ((lane & (PAD - 1)) == (iota((n * PAD, LANES), 0) & (PAD - 1))) & (lane < 2 * PAD)
@@ -215,7 +225,12 @@
             scatter(first_lines, serve)
     scatter(other_lines, serve)
     rows[s] = served[s]
-
+    asked_all[r] = table_in
+    for i in range(1, m):
+        remote(asked_all.at[r], asked_all.at[r], ask_sem, (i,), s, line(i)).start()
+
+    for copy in small_copies[2:]:
+        copy.wait()
     src_row = src_ref[...].reshape(1, E).astype(F32)
     src_hot = rowhot(column(src_row), T)
     dst_hot = rowhot(column(dst_ref[...].reshape(1, E).astype(F32)), T)
@@ -269,6 +284,7 @@
     hd[...] = mm(dst_hot, fetched).astype(BF16)
     others(groups[0], lambda ref, w, i: finish(ref, wc_sem.at[1, w, i]))
     wide = 2 * LANES
+    sent = []
 
     def delta_copy(to):
         return pltpu.make_async_remote_copy(
@@ -276,9 +292,12 @@
             device_id=(s, to), device_id_type=pl.DeviceIdType.MESH,
         )
 
-    for c in range(D // wide):
+    for c in (1 - r // 2, r // 2):
+        here = pl.ds(pl.multiple_of(c * wide, wide), wide)
+
         def gate(k):
-            return slice(k * D + c * wide, k * D + (c + 1) * wide)
+            return pl.ds(pl.multiple_of(k * D + c * wide, wide), wide)
+
         reset = mm(hd[...], wi[:, gate(0)]) + mm(encode, wt[:, gate(0)]) + mm(hs[...], wh[:, gate(0)])
         update = mm(hd[...], wi[:, gate(1)]) + mm(encode, wt[:, gate(1)]) + mm(hs[...], wh[:, gate(1)])
         reset = 0.5 * jnp.tanh(0.5 * reset) + 0.5
@@ -286,17 +305,18 @@
         fresh = jnp.tanh(
             mm(hd[...], wi[:, gate(2)]) + mm(encode, wt[:, gate(2)]) + reset * mm(hs[...], wh[:, gate(2)])
         )
-        hold = hs[:, c * wide:(c + 1) * wide].astype(F32)
+        hold = hs[:, here].astype(F32)
         change = (1.0 - update) * (fresh - hold)
-        hn[:, c * wide:(c + 1) * wide] = hold + change
+        hn[:, here] = hold + change
         delta = mm(src_hot_t, change.astype(BF16))
         for k in range(2):
-            to = 2 * c + k
-            dsend[to] = (delta[:, k * LANES:(k + 1) * LANES] * share).astype(BF16)
-
-            @pl.when(r != to)
-            def _():
-                delta_copy(to).start()
+            dsend[2 * c + k] = (delta[:, k * LANES:(k + 1) * LANES] * share).astype(BF16)
+        if not sent:
+            delta_copy(line(2)).start()
+            delta_copy(4 * c + 1 - line(2)).start()
+        else:
+            delta_copy(4 * c + 1 - r).start()
+        sent.append(c)
 
     dall[r] = dsend[r]
     for i in range(1, m):
@@ -348,7 +368,7 @@
     blocks = E // BLK
     block_no = iota((BLK, E), 1) >> 7
     for q in range(blocks):
-        times = (block_no == listed_ref[0, q]).astype(F32) + (block_no == listed_ref[1, q]).astype(F32)
+        times = sum((block_no == listed_ref[k:k + 1, q:q + 1]).astype(F32) for k in range(2))
         seen = times > 0.0
         for h in range(H):
             cols = slice(h * head, (h + 1) * head)
@@ -360,6 +380,9 @@
             prob = (weighed / jnp.sum(weighed, axis=1, keepdims=True)).astype(BF16)
             attend = mm(prob, keyval[:, D + h * head:D + (h + 1) * head])
             embed_ref[at, cols] = (hn[at, cols] + attend).astype(BF16)
+
+    embed_copy = pltpu.make_async_copy(embed_ref, embed_hbm, local_sem.at[1])
+    embed_copy.start()
 
     def cols_of(rep):
         return pl.ds(pl.multiple_of(rep * LANES, LANES), LANES)
@@ -401,6 +424,7 @@
         finish(newcol.at[pl.ds(0, step)], new_sem.at[1, 1 - c % 2, c])
         finish(newcol.at[pl.ds(0, step)], new_sem.at[1, 2 + c % 2, c])
 
+    embed_copy.wait()
     finish(halfway.at[pl.ds(0, YS - 1)], req_sem.at[0, 0])
     finish(asked.at[:, pl.ds(0, W - 1)], req_sem.at[0, 1])
     for turn in turns:
@@ -448,16 +472,21 @@
     R, D = memory.shape
     cap = 2 * T // n + 2
     G = m * cap
-    vmem = pl.BlockSpec(memory_space=pltpu.VMEM)
     anywhere = pl.BlockSpec(memory_space=pl.ANY)
     weights = (w_input, w_time, w_hidden, w_query, w_keyval)
     dma = pltpu.SemaphoreType.DMA
+    small = (
+        touch_owner.reshape(1, T), touch_row.reshape(1, T), touch_time.reshape(1, T),
+        src_slot, dst_slot, event_time,
+        neighbour_blocks.T, time_freq.reshape(1, -1), time_phase.reshape(1, -1),
+    )
     embed, new_memory = pl.pallas_call(
         functools.partial(body, n, m, cap),
         out_shape=(jax.ShapeDtypeStruct((E, D), BF16), jax.ShapeDtypeStruct((R, D), BF16)),
-        in_specs=[vmem] * 6 + [pl.BlockSpec(memory_space=pltpu.SMEM)] + [vmem] * 2 + [anywhere] * 6,
-        out_specs=(vmem, anywhere),
-        scratch_shapes=[pltpu.VMEM((R, D), BF16)]
+        in_specs=[anywhere] * 15,
+        out_specs=(anywhere, anywhere),
+        scratch_shapes=[pltpu.VMEM(x.shape, x.dtype) for x in small]
+        + [dma((len(small),)), pltpu.VMEM((E, D), BF16), pltpu.VMEM((R, D), BF16)]
         + [pltpu.VMEM((w.shape[0], w.shape[1] * m), BF16) for w in weights]
         + [
             pltpu.VMEM((YS, n // YS, 1, LANES), F32),
@@ -495,9 +524,7 @@
             collective_id=0, has_side_effects=True, vmem_limit_bytes=56 * 1024 * 1024
         ),
     )(
-        touch_owner.reshape(1, T), touch_row.reshape(1, T), touch_time.reshape(1, T),
-        src_slot, dst_slot, event_time,
-        neighbour_blocks.T, time_freq.reshape(1, -1), time_phase.reshape(1, -1),
+        *small,
         memory, *weights,
     )
     return pl.pallas_call(

time: 96.6 us -> 94.8 us (0.981)
  Pallas kernels: 95.6 us -> 93.9 us
    pallas_call x1, Pallas kernels: 93.5 us -> 91.7 us  [shards(): pl.pallas_call(functools.partial(body, n, m, cap), out_shape=(jax.ShapeDt...]
where the time goes in v3:
time: 94.8 us; the launch traced here: 94.7 us
  Pallas kernels  93.9 us (99%)
    pallas_call x1, Pallas kernels, shards(): pl.pallas_call(functools.partial(body, n, m, cap), out_shape=(jax.ShapeDt...  91.7 us
    pallas_call x1, Pallas kernels, shards(): pl.pallas_call(settle, out_shape=(jax.ShapeDtypeStruct((E, D), BF16), jax...  2.14 us

profile of v3, /device:TPU:1, one launch (start us, length us, event | category | flops | bytes accessed | tf_op | source)
XLA Modules:
  0.0 94.7 jit_solution(14627916089125808335)
XLA Ops:
  0.6 91.7 %shard_map.158 = (bf16[384,512]{1,0:T(8,128)(2,1)}, bf16[1024,512]{1,0:T(8,128)(2,1)}) custom-call(s32[1,256]{1,0:T(1,128)} %bitcast.6, s32[1,256]{1,0:T(1,128)} %bitcast.7, s32[1,256]{1,0:T(1,128)} %bitcast.8, s32[384]{0:T(512)} %refs_3_.1, s32[384]{0:T(512)} %refs_4_.1, s32[384]{0:T(512)} %refs_5_.1, s32[2,3]{1,0:T(2,128)} %bitcast.9, f32[1,128]{1,0:T(1,128)} %bitcast.10, ...), custom_call_target="tpu_custom_call" | custom-call | tf_op jit(solution)/shard_map/pallas_call | solution.py:483
  92.4 2.1 %shard_map.159 = (bf16[384,512]{1,0:T(8,128)(2,1)}, bf16[1024,512]{1,0:T(8,128)(2,1)}) custom-call(bf16[384,512]{1,0:T(8,128)(2,1)} %get-tuple-element.4.embed_in, bf16[1024,512]{1,0:T(8,128)(2,1)} %get-tuple-element.5.new_in), custom_call_target="tpu_custom_call" | custom-call | bytes 2883584 | tf_op jit(solution)/shard_map/pallas_call | solution.py:530

commit v4 on v3

--- a/solution.py
+++ b/solution.py
@@ -63,7 +63,7 @@
     (
     mem, wi, wt, wh, wq, wk,
     reqbuf, halfway, asked, asked_all, slots_all, served, rows, place_hot, owner_hot,
-    hs, hd, hn, dsend, dall, outbuf, landed, newcol, want, slot_hot, total,
+    hs, hd, hn, dsend, dall, outbuf, landed, newcol, slot_hot, total,
     local_sem, req_sem, slot_sem, ask_sem, wx_sem, wc_sem, row_sem, delta_sem, out_sem, new_sem,
     ) = refs
     s = lax.axis_index("shard")
@@ -94,17 +94,6 @@
     for copy in small_copies:
         copy.start()
     weights = ((wi_hbm, wi), (wt_hbm, wt), (wh_hbm, wh), (wq_hbm, wq), (wk_hbm, wk))
-    mem_copy = pltpu.make_async_copy(mem_hbm, mem, local_sem.at[0])
-    mem_copy.start()
-    own = []
-    for at, (shard_ref, full) in enumerate(weights):
-        width = shard_ref.shape[1]
-        copy = pltpu.make_async_copy(
-            shard_ref, full.at[:, pl.ds(pl.multiple_of(r * width, LANES), width)], local_sem.at[1 + at]
-        )
-        copy.start()
-        own.append(copy)
-
     barrier = pltpu.get_barrier_semaphore()
 
     yy = s // W
@@ -171,6 +160,16 @@
     for i in range(1, YS):
         y = lax.rem(yy + i, YS)
         remote(reqbuf.at[y], halfway.at[yy], req_sem, (0,), y * W + ww, r).start()
+    mem_copy = pltpu.make_async_copy(mem_hbm, mem, local_sem.at[0])
+    mem_copy.start()
+    own = []
+    for at, (shard_ref, full) in enumerate(weights):
+        width = shard_ref.shape[1]
+        copy = pltpu.make_async_copy(
+            shard_ref, full.at[:, pl.ds(pl.multiple_of(r * width, LANES), width)], local_sem.at[1 + at]
+        )
+        copy.start()
+        own.append(copy)
     finish(halfway.at[pl.ds(0, YS - 1)], req_sem.at[1, 0])
 
     def ask(i, carry):
@@ -204,28 +203,28 @@
 
     finish(asked.at[:, pl.ds(0, W - 1)], req_sem.at[1, 1])
     table_in = asked[...].reshape(n, LANES)
-    spread = one_hot((iota((n * PAD, n), 0) >> 3) == iota((n * PAD, n), 1))
-    lane = iota((n * PAD, LANES), 1)
-    mine = ((lane & (PAD - 1)) == (iota((n * PAD, LANES), 0) & (PAD - 1))) & (lane < 2 * PAD)
-    picked = jnp.where(mine, mm(spread, table_in.astype(BF16)), 0.0).astype(BF16)
+    table_in = table_in.astype(BF16)
     depth_at = iota((LANES, LANES), 0)
     scale = jnp.where(depth_at < PAD, 32.0, jnp.where(depth_at < 2 * PAD, 1.0, 0.0)).astype(BF16)
-    want[...] = mm(picked, scale) - 1.0
+    piece = 2 * W * PAD
+    lane = iota((piece, LANES), 1)
+    mine = ((lane & (PAD - 1)) == (iota((piece, LANES), 0) & (PAD - 1))) & (lane < 2 * PAD)
     mem_copy.wait()
-    piece = 2 * W * PAD
 
     def serve(turn, to):
         remote(served.at[to, pl.ds(0, cap)], rows.at[s, pl.ds(0, cap)], row_sem, (turn,), to, r).start()
 
     for turn in turns:
         first = quarter(turn) * 2 * W
-        hot = rowhot(want[pl.ds(pl.multiple_of(first * PAD, piece), piece)], R)
+        spread = one_hot((iota((piece, n), 0) >> 3) + first == iota((piece, n), 1))
+        picked = jnp.where(mine, mm(spread, table_in), 0.0).astype(BF16)
+        hot = rowhot(mm(picked, scale) - 1.0, R)
         served[pl.ds(first, 2 * W)] = mm(hot, mem[...]).astype(BF16).reshape(2 * W, PAD, D)
         if turn == turns[0]:
             scatter(first_lines, serve)
     scatter(other_lines, serve)
     rows[s] = served[s]
-    asked_all[r] = table_in
+    asked_all[r] = asked[...].reshape(n, LANES)
     for i in range(1, m):
         remote(asked_all.at[r], asked_all.at[r], ask_sem, (i,), s, line(i)).start()
 
@@ -321,7 +320,6 @@
     dall[r] = dsend[r]
     for i in range(1, m):
         finish(dall.at[0], delta_sem.at[1, line(i)])
-    give(groups[1])
 
     def post(turn, to):
         remote(outbuf.at[to], landed.at[s], out_sem, (turn,), to, r).start()
@@ -334,6 +332,7 @@
         if turn == turns[0]:
             scatter(first_lines, post)
     scatter(other_lines, post)
+    give(groups[1])
     landed[s] = outbuf[s]
 
     for i in range(1, m):
@@ -506,7 +505,6 @@
             pltpu.VMEM((n, G, LANES), BF16),
             pltpu.VMEM((n, G, LANES), BF16),
             pltpu.VMEM((R, LANES), BF16),
-            pltpu.VMEM((n * PAD, LANES), F32),
             pltpu.VMEM((T, n * PAD), BF16),
             pltpu.VMEM((R, LANES), F32),
             dma((6,)),

time: 94.8 us -> 94.6 us (level)
  no operation moved by 1% of the time
where the time goes in v4:
time: 94.6 us; the launch traced here: 94.4 us
  Pallas kernels  93.6 us (99%)
    pallas_call x1, Pallas kernels, shards(): pl.pallas_call(functools.partial(body, n, m, cap), out_shape=(jax.ShapeDt...  91.5 us
    pallas_call x1, Pallas kernels, shards(): pl.pallas_call(settle, out_shape=(jax.ShapeDtypeStruct((E, D), BF16), jax...  2.14 us

profile of v4, /device:TPU:1, one launch (start us, length us, event | category | flops | bytes accessed | tf_op | source)
XLA Modules:
  0.0 94.4 jit_solution(17368229270467504039)
XLA Ops:
  0.6 91.5 %shard_map.158 = (bf16[384,512]{1,0:T(8,128)(2,1)}, bf16[1024,512]{1,0:T(8,128)(2,1)}) custom-call(s32[1,256]{1,0:T(1,128)} %bitcast.6, s32[1,256]{1,0:T(1,128)} %bitcast.7, s32[1,256]{1,0:T(1,128)} %bitcast.8, s32[384]{0:T(512)} %refs_3_.1, s32[384]{0:T(512)} %refs_4_.1, s32[384]{0:T(512)} %refs_5_.1, s32[2,3]{1,0:T(2,128)} %bitcast.9, f32[1,128]{1,0:T(1,128)} %bitcast.10, ...), custom_call_target="tpu_custom_call" | custom-call | tf_op jit(solution)/shard_map/pallas_call | solution.py:482
  92.1 2.1 %shard_map.159 = (bf16[384,512]{1,0:T(8,128)(2,1)}, bf16[1024,512]{1,0:T(8,128)(2,1)}) custom-call(bf16[384,512]{1,0:T(8,128)(2,1)} %get-tuple-element.4.embed_in, bf16[1024,512]{1,0:T(8,128)(2,1)} %get-tuple-element.5.new_in), custom_call_target="tpu_custom_call" | custom-call | bytes 2883584 | tf_op jit(solution)/shard_map/pallas_call | solution.py:528

commit v5 on v4

--- a/solution.py
+++ b/solution.py
@@ -13,7 +13,7 @@
 LANES = 128
 PAD = 8
 YS = 8
-CUTS = 8
+CUTS = 16
 F32 = jnp.float32
 BF16 = jnp.bfloat16
 I32 = jnp.int32

time: 94.6 us -> 95 us (level)
  no operation moved by 1% of the time
where the time goes in v5:
time: 95 us; the launch traced here: 94.8 us
  Pallas kernels  94 us (99%)
    pallas_call x1, Pallas kernels, shards(): pl.pallas_call(functools.partial(body, n, m, cap), out_shape=(jax.ShapeDt...  91.9 us
    pallas_call x1, Pallas kernels, shards(): pl.pallas_call(settle, out_shape=(jax.ShapeDtypeStruct((E, D), BF16), jax...  2.14 us

profile of v5, /device:TPU:1, one launch (start us, length us, event | category | flops | bytes accessed | tf_op | source)
XLA Modules:
  0.0 94.8 jit_solution(9459686400828913339)
XLA Ops:
  0.6 91.9 %shard_map.158 = (bf16[384,512]{1,0:T(8,128)(2,1)}, bf16[1024,512]{1,0:T(8,128)(2,1)}) custom-call(s32[1,256]{1,0:T(1,128)} %bitcast.6, s32[1,256]{1,0:T(1,128)} %bitcast.7, s32[1,256]{1,0:T(1,128)} %bitcast.8, s32[384]{0:T(512)} %refs_3_.1, s32[384]{0:T(512)} %refs_4_.1, s32[384]{0:T(512)} %refs_5_.1, s32[2,3]{1,0:T(2,128)} %bitcast.9, f32[1,128]{1,0:T(1,128)} %bitcast.10, ...), custom_call_target="tpu_custom_call" | custom-call | tf_op jit(solution)/shard_map/pallas_call | solution.py:482
  92.5 2.1 %shard_map.159 = (bf16[384,512]{1,0:T(8,128)(2,1)}, bf16[1024,512]{1,0:T(8,128)(2,1)}) custom-call(bf16[384,512]{1,0:T(8,128)(2,1)} %get-tuple-element.4.embed_in, bf16[1024,512]{1,0:T(8,128)(2,1)} %get-tuple-element.5.new_in), custom_call_target="tpu_custom_call" | custom-call | bytes 2883584 | tf_op jit(solution)/shard_map/pallas_call | solution.py:528
